TPU v7x, 32 devices: a whole 2x2x4 slice. The times are simulated.
32 devices in a mesh: groups: 2 (over y), seq: 4 (over z), mp: 4 (over x, core).
Axes of the slice: x: 2, y: 2, z: 4, core: 2. Of those that a mesh axis runs over, the one named last changes fastest.
Arguments:
- node_vectors: bfloat16 [1024, 2048], P(('groups', 'seq'), 'mp'), parts along dimension 0, may hold values from -6 to 6
- standardize_multiplier: float32 [2048], replicated, may hold values from 0.1 to 1.9
- probe_matrix: bfloat16 [2048, 1024], P(None, 'mp'), may hold values from -1 to 1
- lookup_matrix: bfloat16 [2048, 1024], P(None, 'mp'), may hold values from -1 to 1
- content_matrix: bfloat16 [2048, 1024], P(None, 'mp'), may hold values from -0.125 to 0.125
- softness_per_group: float32 [8], P('mp'), may hold values from 0.5 to 12
- exit_matrix: bfloat16 [1024, 2048], P('mp'), may hold values from -0.1875 to 0.1875
Outputs:
- mixed: bfloat16 [1024, 2048], P(('groups', 'seq'), 'mp'), parts along dimension 0
There are 2 independent parts, one for each index of `groups`. A program takes and returns all parts, laid end to end along the dimension named above; an argument that names none is the same for every part. Nothing has to cross between parts.
All inputs are finite; a program needn't handle non-finite values.
Results may differ from a plain program's by a relative error of at most 0.011.
Values may be sent and summed in bfloat16 or wider, within the bound.
A program may use at most 64 MiB of HBM per device.

v0:
```python
import math
import jax
import jax.numpy as jnp
from jax import lax
from jax.sharding import PartitionSpec as P


def attend(state_in, blocks, query_heads, inverse_root_span, resident_groups, channel_span):
    running_max, running_sum, weighted = state_in
    key_block, value_block = blocks
    count = key_block.shape[0]
    key_heads = key_block.reshape(count, resident_groups, channel_span)
    value_heads = value_block.reshape(count, resident_groups, channel_span)
    scores = (
        jnp.einsum("rhd,nhd->hrn", query_heads, key_heads, preferred_element_type=jnp.float32)
        * inverse_root_span[:, None, None]
    )
    new_max = jnp.max(scores, axis=-1)
    rescale = jnp.exp(running_max - new_max)
    weights = jnp.exp(scores - new_max[:, :, None])
    running_sum = running_sum * rescale + jnp.sum(weights, axis=-1)
    update = jnp.einsum(
        "hrn,nhd->hrd",
        weights.astype(jnp.bfloat16),
        value_heads,
        preferred_element_type=jnp.float32,
    )
    weighted = weighted * rescale[:, :, None] + update
    return (new_max, running_sum, weighted)


def per_device(
    node_vectors,
    standardize_multiplier,
    probe_matrix,
    lookup_matrix,
    content_matrix,
    softness_per_group,
    exit_matrix,
):
    full_rows = lax.all_gather(node_vectors, "mp", axis=1, tiled=True)
    widened = full_rows.astype(jnp.float32)
    average = jnp.mean(widened, axis=-1, keepdims=True)
    centered = widened - average
    variance = jnp.mean(centered * centered, axis=-1, keepdims=True)
    normed = (centered * lax.rsqrt(variance + 1e-05) * standardize_multiplier).astype(jnp.bfloat16)
    queries = jnp.dot(normed, probe_matrix, preferred_element_type=jnp.float32).astype(jnp.bfloat16)
    key_rows = jnp.dot(normed, lookup_matrix, preferred_element_type=jnp.float32).astype(
        jnp.bfloat16
    )
    value_rows = jnp.dot(normed, content_matrix, preferred_element_type=jnp.float32).astype(
        jnp.bfloat16
    )
    resident_groups = softness_per_group.shape[0]
    head_cols = queries.shape[1]
    channel_span = head_cols // resident_groups
    token_count = queries.shape[0]
    query_heads = queries.reshape(token_count, resident_groups, channel_span)
    inverse_root_span = softness_per_group / math.sqrt(channel_span)
    initial = (
        jnp.full((resident_groups, token_count), -jnp.inf, jnp.float32),
        jnp.zeros((resident_groups, token_count), jnp.float32),
        jnp.zeros((resident_groups, token_count, channel_span), jnp.float32),
    )
    final = attend(
        initial,
        (
            lax.all_gather(key_rows, "seq", axis=0, tiled=True),
            lax.all_gather(value_rows, "seq", axis=0, tiled=True),
        ),
        query_heads,
        inverse_root_span,
        resident_groups,
        channel_span,
    )
    heads_out = (
        (final[2] / final[1][:, :, None])
        .transpose(1, 0, 2)
        .reshape(token_count, head_cols)
        .astype(jnp.bfloat16)
    )
    partial_sums = jnp.dot(heads_out, exit_matrix, preferred_element_type=jnp.float32)
    summed = lax.psum_scatter(
        partial_sums.astype(jnp.bfloat16), "mp", scatter_dimension=1, tiled=True
    ).astype(jnp.float32)
    return (node_vectors.astype(jnp.float32) + summed).astype(jnp.bfloat16)


def solution(mesh):
    return jax.shard_map(
        per_device,
        mesh=mesh,
        in_specs=(
            P(("groups", "seq"), "mp"),
            P(),
            P(None, "mp"),
            P(None, "mp"),
            P(None, "mp"),
            P("mp"),
            P("mp", None),
        ),
        out_specs=P(("groups", "seq"), "mp"),
        check_vma=False,
    )
```

profile of v0, /device:TPU:0, one launch (start us, length us, event | category | flops | bytes accessed | tf_op | source)
XLA Modules:
  0.0 81.6 jit_solution(14585379958456140718)
XLA Ops:
  6.5 0.0 copy-start
  6.5 0.0 copy-start.2
  6.5 0.0 reduce-scatter.2.cloned.1.call-start
  6.5 0.8 broadcast_multiply_fusion
  7.3 8.8 %all_gather.9 = bf16[128,2048]{1,0:T(8,128)(2,1)S(1)} all-gather(bf16[128,512]{1,0:T(8,128)(2,1)} %param.7), channel_id=1, replica_groups=mesh['groups'=2,'seq'=4,'mp'=4] {'mp'}, dimensions={1}, use_global_device_ids=true | all-gather | bytes 655360 | tf_op jit(solution)/shard_map/all_gather | solution.py:41
  16.2 0.2 convert_reduce_fusion
  16.4 0.0 copy-start.5
  16.4 0.3 fusion.6
  16.7 0.0 copy-done.2
  16.7 0.4 copy-done.5
  17.1 0.0 copy-start.3
  17.1 0.4 convolution_convert_fusion.2
  17.4 0.9 %copy-done.3 = bf16[2048,256]{1,0:T(8,128)(2,1)S(1)} copy-done((bf16[2048,256]{1,0:T(8,128)(2,1)S(1)}, bf16[2048,256]{1,0:T(8,128)(2,1)}, u32[]{:S(2)}) %copy-start.3) | copy-done | bytes 1048600
  18.3 0.0 copy-start.4
  18.3 0.4 convolution_convert_fusion.1
  18.6 0.9 %copy-done.4 = bf16[2048,256]{1,0:T(8,128)(2,1)S(1)} copy-done((bf16[2048,256]{1,0:T(8,128)(2,1)S(1)}, bf16[2048,256]{1,0:T(8,128)(2,1)}, u32[]{:S(2)}) %copy-start.4) | copy-done | bytes 1048600
  19.5 0.4 fusion.5
  19.9 14.1 %all_gather.11 = bf16[512,256]{1,0:T(8,128)(2,1)S(1)} all-gather(bf16[128,256]{1,0:T(8,128)(2,1)S(1)} %convolution_convert_fusion.1), channel_id=1, replica_groups=mesh['groups'=2,'seq'=4,'mp'=4] {'seq'}, dimensions={0}, use_global_device_ids=true | all-gather | bytes 327680 | tf_op jit(solution)/shard_map/all_gather | solution.py:69
  34.0 0.1 copy.11
  34.1 14.6 %all_gather.10 = bf16[512,256]{1,0:T(8,128)(2,1)S(1)} all-gather(bf16[128,256]{1,0:T(8,128)(2,1)S(1)} %convolution_convert_fusion.2), channel_id=1, replica_groups=mesh['groups'=2,'seq'=4,'mp'=4] {'seq'}, dimensions={0}, use_global_device_ids=true | all-gather | bytes 327680 | tf_op jit(solution)/shard_map/all_gather | solution.py:68
  48.7 0.3 fusion.20
  49.1 0.2 fusion.9
  49.3 0.3 fusion.4
  49.6 0.0 copy-done
  49.6 1.1 %convolution_convert_fusion = bf16[128,2048]{1,0:T(8,128)(2,1)} fusion(bf16[128,256]{0,1:T(8,128)(2,1)S(1)} %bitcast.39, bf16[256,2048]{1,0:T(8,128)(2,1)S(1)} %copy-done), kind=kOutput, calls=%fused_computation | convolution fusion | flops 134479872 | bytes 1638400 | tf_op jit(solution)/shard_map/dot_general | solution.py:82
  50.8 0.0 copy-start.1
  50.8 0.0 reduce-scatter.2.cloned.1.call-update
  50.8 22.4 %reduce-scatter.2.cloned.1.call-done = bf16[128,512]{1,0:T(8,128)(2,1)} async-done(((bf16[128,2048]{1,0:T(8,128)(2,1)}), bf16[128,512]{1,0:T(8,128)(2,1)}) %reduce-scatter.2.cloned.1.call-update) | async-done | bytes 131088 | tf_op jit(solution)/shard_map/reduce_scatter | solution.py:83
  73.2 0.0 copy-done.1
  73.2 1.6 %add_convert_fusion = bf16[128,512]{1,0:T(8,128)(2,1)} fusion(bf16[128,512]{1,0:T(8,128)(2,1)} %reduce-scatter.2.cloned.1.call-done, bf16[128,512]{1,0:T(8,128)(2,1)S(1)} %copy-done.1), kind=kLoop, calls=%fused_computation.22 | loop fusion | flops 262144 | bytes 393216 | tf_op jit(solution)/shard_map/convert_element_type | solution.py:86
  (4 shorter events, 0.0 us)
Async XLA Ops:
  6.5 43.1 %copy-start = (bf16[256,2048]{1,0:T(8,128)(2,1)S(1)}, bf16[256,2048]{1,0:T(8,128)(2,1)}, u32[]{:S(2)}) copy-start(bf16[256,2048]{1,0:T(8,128)(2,1)} %param.13) | copy-start | bytes 3145732
  6.5 10.1 %copy-start.2 = (bf16[2048,256]{1,0:T(8,128)(2,1)S(1)}, bf16[2048,256]{1,0:T(8,128)(2,1)}, u32[]{:S(2)}) copy-start(bf16[2048,256]{1,0:T(8,128)(2,1)} %param.10) | copy-start | bytes 3145732
  6.5 66.6 %reduce-scatter.2.cloned.1.call-start = ((), (), s32[]{:S(2)}) async-start(), calls=%async_computation.1 | async-start | bytes 655360 | tf_op jit(solution)/shard_map/reduce_scatter | solution.py:83
  16.4 0.7 copy-start.5
  17.1 1.2 %copy-start.3 = (bf16[2048,256]{1,0:T(8,128)(2,1)S(1)}, bf16[2048,256]{1,0:T(8,128)(2,1)}, u32[]{:S(2)}) copy-start(bf16[2048,256]{1,0:T(8,128)(2,1)} %param.11) | copy-start | bytes 3145732
  18.3 1.2 %copy-start.4 = (bf16[2048,256]{1,0:T(8,128)(2,1)S(1)}, bf16[2048,256]{1,0:T(8,128)(2,1)}, u32[]{:S(2)}) copy-start(bf16[2048,256]{1,0:T(8,128)(2,1)} %param.9) | copy-start | bytes 3145732
  50.8 22.4 %copy-start.1 = (bf16[128,512]{1,0:T(8,128)(2,1)S(1)}, bf16[128,512]{1,0:T(8,128)(2,1)}, u32[]{:S(2)}) copy-start(bf16[128,512]{1,0:T(8,128)(2,1)} %param.7) | copy-start | bytes 393220
Sparse Core Ops, SparseCore 0:
  50.9 22.2 reduce-scatter.1
where the time goes:
time: 81.9 us; the launch traced here: 81.6 us
  blocking collectives  37.6 us (46%)
  waiting for transfers between devices  22.4 us (27%)
  between operations  13.5 us (16%)
  other arithmetic  3.1 us (4%)
  matrix products  2.85 us (3%)
  local copies, waits for them, and re-layouts  2.25 us (3%)
    reduce_scatter x1, waiting for transfers between devices, per_device(): lax.psum_scatter(partial_sums.astype(jnp.bfloat16), 'mp', scatter_dimensi...  22.4 us
    all_gather x1, blocking collectives, per_device(): lax.all_gather(key_rows, 'seq', axis=0, tiled=True)  14.6 us
    all_gather x1, blocking collectives, per_device(): lax.all_gather(value_rows, 'seq', axis=0, tiled=True)  14.1 us
    all_gather x1, blocking collectives, per_device(): full_rows = lax.all_gather(node_vectors, 'mp', axis=1, tiled=True)  8.84 us
    unnamed x12, local copies, waits for them, and re-layouts  2.11 us
  transfers between devices with their start and end apart: 1, of which 1 were waited for; matrix products, arithmetic and copies ran while one was open for 0% of the time, Pallas kernels for 0%

commit v1 on v0

--- a/solution.py
+++ b/solution.py
@@ -1,8 +1,21 @@
+import functools
 import math
 import jax
 import jax.numpy as jnp
 from jax import lax
 from jax.sharding import PartitionSpec as P
+
+
+def change_the_clusters(arr, row_axis):
+    queue = []
+    for _ in range(lax.psum(1, row_axis)):
+        queue.append(arr)
+    long_array = jnp.stack(queue, axis=0)
+    base_arr = jnp.concatenate(lax.all_to_all(long_array, row_axis, 0, 0), axis=0)
+    return base_arr
+
+
+_begin_array = functools.partial(change_the_clusters, row_axis="seq")
 
 
 def attend(state_in, blocks, query_heads, inverse_root_span, resident_groups, channel_span):
@@ -64,10 +77,7 @@
     )
     final = attend(
         initial,
-        (
-            lax.all_gather(key_rows, "seq", axis=0, tiled=True),
-            lax.all_gather(value_rows, "seq", axis=0, tiled=True),
-        ),
+        (lax.all_gather(key_rows, "seq", axis=0, tiled=True), _begin_array(value_rows)),
         query_heads,
         inverse_root_span,
         resident_groups,

time: 81.9 us -> 72.5 us (0.89)
  blocking collectives: 37.6 us -> 24.7 us
  starting transfers between devices: 0.01 us -> 5 us
  waiting for transfers between devices: 22.4 us -> 21.4 us
    all_gather x1 -> x0, blocking collectives: 14.1 us -> none  [per_device(): lax.all_gather(value_rows, 'seq', axis=0, tiled=True)]
    all_to_all x0 -> x1, starting transfers between devices: none -> 5 us  [change_the_clusters(): lax.all_to_all(long_array, row_axis, 0, 0)]
    all_gather x1, blocking collectives: 14.6 us -> 15.8 us  [per_device(): lax.all_gather(key_rows, 'seq', axis=0, tiled=True)]
    reduce_scatter x1, waiting for transfers between devices: 22.4 us -> 21.4 us  [per_device(): lax.psum_scatter(partial_sums.astype(jnp.bfloat16), 'mp', scatter_dimensi...]
    unnamed x12 -> x14, local copies, waits for them, and re-layouts: 2.11 us -> 1.25 us
    another operation x0 -> x2, local copies, waits for them, and re-layouts: none -> 0.84 us  [the longest x1 0.73 us: change_the_clusters(): long_array = jnp.stack(queue, axis=0)]
  transfers between devices with their start and end apart: 1 -> 2, of which waited for: 1 -> 1; matrix products, arithmetic and copies ran while one was open for 0% -> 2% of each run, Pallas kernels for 0% -> 0%
where the time goes in v1:
time: 72.5 us; the launch traced here: 72.2 us
  blocking collectives  24.7 us (34%)
  waiting for transfers between devices  21.4 us (30%)
  between operations  13.5 us (19%)
  starting transfers between devices  5 us (7%)
  matrix products  2.86 us (4%)
  local copies, waits for them, and re-layouts  2.41 us (3%)
  other arithmetic  2.3 us (3%)
    reduce_scatter x1, waiting for transfers between devices, per_device(): lax.psum_scatter(partial_sums.astype(jnp.bfloat16), 'mp', scatter_dimensi...  21.4 us
    all_gather x1, blocking collectives, per_device(): lax.all_gather(key_rows, 'seq', axis=0, tiled=True)  15.8 us
    all_gather x1, blocking collectives, per_device(): full_rows = lax.all_gather(node_vectors, 'mp', axis=1, tiled=True)  8.97 us
    all_to_all x1, starting transfers between devices, change_the_clusters(): lax.all_to_all(long_array, row_axis, 0, 0)  5 us
    convert_element_type x1, other arithmetic, per_device(): return (node_vectors.astype(jnp.float32) + summed).astype(jnp.bfloat16)  1.59 us
  transfers between devices with their start and end apart: 2, of which 1 were waited for; matrix products, arithmetic and copies ran while one was open for 2% of the time, Pallas kernels for 0%

profile of v1, /device:TPU:0, one launch (start us, length us, event | category | flops | bytes accessed | tf_op | source)
XLA Modules:
  0.0 72.2 jit_solution(7887713855276321991)
XLA Ops:
  6.5 0.0 copy-start
  6.5 0.0 copy-start.2
  6.5 9.0 %all_gather.6 = bf16[128,2048]{1,0:T(8,128)(2,1)S(1)} all-gather(bf16[128,512]{1,0:T(8,128)(2,1)} %param.7), channel_id=1, replica_groups=mesh['groups'=2,'seq'=4,'mp'=4] {'mp'}, dimensions={1}, use_global_device_ids=true | all-gather | bytes 655360 | tf_op jit(solution)/shard_map/all_gather | solution.py:54
  15.5 0.2 convert_reduce_fusion
  15.7 0.0 copy-start.5
  15.7 0.3 fusion.6
  16.0 0.0 copy-done.2
  16.0 0.4 copy-done.5
  16.4 0.0 copy-start.3
  16.4 0.4 convolution_convert_fusion.1
  16.8 0.1 copy.13
  16.9 0.7 %stack.2 = bf16[4,128,256]{1,2,0:T(8,128)(2,1)} broadcast(bf16[128,256]{0,1:T(8,128)(2,1)S(1)} %copy.13), dimensions={1,2} | broadcast | bytes 327680 | tf_op jit(solution)/shard_map/stack | solution.py:13
  17.6 0.0 copy-start.6
  17.6 5.0 %all-to-all-start = ((bf16[4,128,256]{1,2,0:T(8,128)(2,1)}), bf16[4,128,256]{1,2,0:T(8,128)(2,1)S(1)}, u32[]{:S(2)}, u32[]{:S(2)}) async-start(bf16[4,128,256]{1,2,0:T(8,128)(2,1)} %stack.2), calls=%async_computation | async-start | bytes 524288 | tf_op jit(solution)/shard_map/all_to_all | solution.py:14
  22.6 0.0 reduce-scatter.2.cloned.1.call-start
  22.6 0.0 copy-done.6
  22.6 0.0 copy-done.3
  22.6 0.0 copy-start.4
  22.6 0.4 convolution_convert_fusion.2
  23.0 0.8 %copy-done.4 = bf16[2048,256]{1,0:T(8,128)(2,1)S(1)} copy-done((bf16[2048,256]{1,0:T(8,128)(2,1)S(1)}, bf16[2048,256]{1,0:T(8,128)(2,1)}, u32[]{:S(2)}) %copy-start.4) | copy-done | bytes 1048600
  23.9 0.4 fusion.5
  24.2 15.8 %all_gather.7 = bf16[512,256]{1,0:T(8,128)(2,1)S(1)} all-gather(bf16[128,256]{1,0:T(8,128)(2,1)S(1)} %convolution_convert_fusion.2), channel_id=1, replica_groups=mesh['groups'=2,'seq'=4,'mp'=4] {'seq'}, dimensions={0}, use_global_device_ids=true | all-gather | bytes 327680 | tf_op jit(solution)/shard_map/all_gather | solution.py:80
  40.0 0.3 fusion.20
  40.3 0.2 fusion.9
  40.5 0.0 all-to-all-done
  40.6 0.2 copy.14
  40.8 0.1 reshape_reshape.3
  40.9 0.3 fusion.4
  41.2 0.0 copy-done
  41.2 1.1 %convolution_convert_fusion = bf16[128,2048]{1,0:T(8,128)(2,1)} fusion(bf16[128,256]{0,1:T(8,128)(2,1)S(1)} %bitcast.39, bf16[256,2048]{1,0:T(8,128)(2,1)S(1)} %copy-done), kind=kOutput, calls=%fused_computation | convolution fusion | flops 134479872 | bytes 1638400 | tf_op jit(solution)/shard_map/dot_general | solution.py:92
  42.3 0.0 copy-start.1
  42.3 0.0 reduce-scatter.2.cloned.1.call-update
  42.4 21.4 %reduce-scatter.2.cloned.1.call-done = bf16[128,512]{1,0:T(8,128)(2,1)} async-done(((bf16[128,2048]{1,0:T(8,128)(2,1)}), bf16[128,512]{1,0:T(8,128)(2,1)}) %reduce-scatter.2.cloned.1.call-update) | async-done | bytes 131088 | tf_op jit(solution)/shard_map/reduce_scatter | solution.py:93
  63.7 0.0 copy-done.1
  63.8 1.6 %add_convert_fusion = bf16[128,512]{1,0:T(8,128)(2,1)} fusion(bf16[128,512]{1,0:T(8,128)(2,1)} %reduce-scatter.2.cloned.1.call-done, bf16[128,512]{1,0:T(8,128)(2,1)S(1)} %copy-done.1), kind=kLoop, calls=%fused_computation.22 | loop fusion | flops 262144 | bytes 393216 | tf_op jit(solution)/shard_map/convert_element_type | solution.py:96
  (5 shorter events, 0.0 us)
Async XLA Ops:
  6.5 34.7 %copy-start = (bf16[256,2048]{1,0:T(8,128)(2,1)S(1)}, bf16[256,2048]{1,0:T(8,128)(2,1)}, u32[]{:S(2)}) copy-start(bf16[256,2048]{1,0:T(8,128)(2,1)} %param.13) | copy-start | bytes 3145732
  6.5 9.4 %copy-start.2 = (bf16[2048,256]{1,0:T(8,128)(2,1)S(1)}, bf16[2048,256]{1,0:T(8,128)(2,1)}, u32[]{:S(2)}) copy-start(bf16[2048,256]{1,0:T(8,128)(2,1)} %param.11) | copy-start | bytes 3145732
  15.7 0.7 copy-start.5
  16.4 6.2 %copy-start.3 = (bf16[2048,256]{1,0:T(8,128)(2,1)S(1)}, bf16[2048,256]{1,0:T(8,128)(2,1)}, u32[]{:S(2)}) copy-start(bf16[2048,256]{1,0:T(8,128)(2,1)} %param.10) | copy-start | bytes 3145732
  17.6 5.0 %copy-start.6 = (f32[2]{0:T(128)S(1)}, f32[2]{0:T(128)}, u32[]{:S(2)}) copy-start(f32[2]{0:T(128)} %param.12) | copy-start | bytes 28
  17.6 22.9 %all-to-all-start = ((bf16[4,128,256]{1,2,0:T(8,128)(2,1)}), bf16[4,128,256]{1,2,0:T(8,128)(2,1)S(1)}, u32[]{:S(2)}, u32[]{:S(2)}) async-start(bf16[4,128,256]{1,2,0:T(8,128)(2,1)} %stack.2), calls=%async_computation | async-start | bytes 524288 | tf_op jit(solution)/shard_map/all_to_all | solution.py:14
  22.6 41.1 %reduce-scatter.2.cloned.1.call-start = ((), (), s32[]{:S(2)}) async-start(), calls=%async_computation.2 | async-start | bytes 655360 | tf_op jit(solution)/shard_map/reduce_scatter | solution.py:93
  22.6 1.2 %copy-start.4 = (bf16[2048,256]{1,0:T(8,128)(2,1)S(1)}, bf16[2048,256]{1,0:T(8,128)(2,1)}, u32[]{:S(2)}) copy-start(bf16[2048,256]{1,0:T(8,128)(2,1)} %param.9) | copy-start | bytes 3145732
  42.3 21.4 %copy-start.1 = (bf16[128,512]{1,0:T(8,128)(2,1)S(1)}, bf16[128,512]{1,0:T(8,128)(2,1)}, u32[]{:S(2)}) copy-start(bf16[128,512]{1,0:T(8,128)(2,1)} %param.7) | copy-start | bytes 393220
Sparse Core Ops, SparseCore 0:
  42.5 21.2 reduce-scatter.1
